TPU v7x, 32 devices: a whole 2x2x4 slice. The times are simulated.
32 devices in a mesh: row: 4 (over z), col: 4 (over x, core), layer: 2 (over y).
Axes of the slice: x: 2, y: 2, z: 4, core: 2. Of those that a mesh axis runs over, the one named last changes fastest.
Arguments:
- left_blocks: float32 [4, 2, 4, 4, 128, 128], P('row', 'layer', 'col'), may hold values from -1.2 to 1.2
- right_blocks: float32 [2, 4, 4, 8, 128, 128], P('layer', 'row', 'col'), may hold values from -1.2 to 1.2
- pair_stacks: int32 [4, 4, 2, 4, 3, 32], P('row', 'col', 'layer'), may hold values from 0 to 32, as said below
Outputs:
- product_window: float32 [4, 4, 32, 128, 128], P('row', 'col', 'layer')
Inputs may be any that keep to these rules, and one draw needn't show every extreme that they name: `pair_stacks`: entry 0 of a list holds left slots below 4, entry 1 right slots below 8, entry 2 product blocks below 32; the live triples stand first, every other slot holds (0, 0, 32); some list is live in all 32 slots.
All inputs are finite; a program needn't handle non-finite values.
Results may differ from a plain program's by a relative error of at most 0.0003.
Values sent between devices are 32-bit elements; how exact they have to be, the bound alone decides.
A program may use at most 64 MiB of HBM per device.

v0:
```python
import jax
import jax.numpy as jnp
from jax import lax
from jax.sharding import PartitionSpec as P

OUT_TILE = 32


def multiply(running, left_piece, right_piece, left_slot, right_slot, out_slot):
    first_blocks = jnp.take(left_piece, left_slot, axis=0)
    second_blocks = jnp.take(right_piece, right_slot, axis=0)
    products = jnp.einsum(
        "qxy,qyz->qxz",
        first_blocks,
        second_blocks,
        precision=lax.Precision.HIGHEST,
        preferred_element_type=jnp.float32,
    )
    return running.at[out_slot].add(products, mode="drop")


def piece_term(accumulated, left_piece, right_piece, triples):
    left_slot = triples[0]
    right_slot = triples[1]
    out_slot = triples[2]
    return multiply(accumulated, left_piece, right_piece, left_slot, right_slot, out_slot)


def body(left_blocks, right_blocks, pair_stacks):
    left_local = left_blocks[0, 0]
    right_local = right_blocks[0, :, 0]
    stacks = pair_stacks[0, 0, 0]
    block_width = left_local.shape[-1]
    initial = jnp.zeros((OUT_TILE, block_width, block_width), jnp.float32)
    right_whole = lax.all_gather(right_local, "row", axis=0, tiled=True)
    pieces = lax.all_gather(left_local, "col", axis=0, tiled=True)

    def visit(position, running):
        left_piece = lax.dynamic_index_in_dim(pieces, position, 0, keepdims=False)
        right_piece = lax.dynamic_index_in_dim(right_whole, position, 0, keepdims=False)
        triples = lax.dynamic_index_in_dim(stacks, position, 0, keepdims=False)
        return piece_term(running, left_piece, right_piece, triples)

    accumulated = lax.fori_loop(0, pieces.shape[0], visit, initial)
    reduced = lax.psum_scatter(accumulated, "layer", scatter_dimension=0, tiled=True)
    return reduced[None, None]


def solution(mesh):
    placed = (
        P("row", "layer", "col", None, None, None),
        P("layer", "row", "col", None, None, None),
        P("row", "col", "layer", None, None, None),
    )
    return jax.shard_map(
        body,
        mesh=mesh,
        in_specs=placed,
        out_specs=P("row", "col", "layer", None, None),
        check_vma=False,
    )
```

profile of v0, /device:TPU:0, one launch (start us, length us, event | category | flops | bytes accessed | tf_op | source)
XLA Modules:
  0.0 182.1 jit_solution(6074862939140767157)
XLA Ops:
  6.5 0.0 all-gather.5.cloned.1.call-start
  6.5 0.7 all-gather.5.cloned.1.call-update
  7.3 0.0 all-gather.7.cloned.1.call-start
  7.3 0.7 all-gather.7.cloned.1.call-update
  8.0 0.0 reduce-scatter.2.cloned.1.call-start
  8.1 0.7 copy.9
  8.7 19.6 %all-gather.5.cloned.1.call-done = f32[4,1,1,4,128,128]{5,4,3,2,1,0:T(8,128)} async-done(((f32[1,1,1,4,128,128]{5,4,3,2,1,0:T(8,128)}), f32[4,1,1,4,128,128]{5,4,3,2,1,0:T(8,128)}) %all-gather.5.cloned.1.call-update) | async-done | bytes 1048592 | tf_op jit(solution)/shard_map/all_gather | solution.py:36
  28.4 47.5 %all-gather.7.cloned.1.call-done = f32[4,1,1,8,128,128]{5,4,3,2,1,0:T(8,128)} async-done(((f32[1,1,1,8,128,128]{5,4,3,2,1,0:T(8,128)}), f32[4,1,1,8,128,128]{5,4,3,2,1,0:T(8,128)}) %all-gather.7.cloned.1.call-update) | async-done | bytes 2097168 | tf_op jit(solution)/shard_map/all_gather | solution.py:35
  75.9 1.6 broadcast_in_dim.43
  77.5 66.5 %while.13 = (s32[]{:T(128)}, f32[32,128,128]{2,1,0:T(8,128)}, s32[4,3,32]{2,1,0:T(4,128)S(1)}, f32[4,4,128,128]{3,2,1,0:T(8,128)}, f32[4,8,128,128]{3,2,1,0:T(8,128)}, /*index=5*/s32[]{:T(128)}) while((s32[]{:T(128)}, f32[32,128,128]{2,1,0:T(8,128)}, s32[4,3,32]{2,1,0:T(4,128)S(1)}, f32[4,4,128,128]{3,2,1,0:T(8,128)}, ...), condition=%wide.region_2.3_spmd, body=%wide.region_0.2_spmd.sunk | while | flops 806881984 | bytes 22555224 | solution.py:44
  77.6 1.0 dynamic-slice_bitcast_fusion.5
  78.5 1.1 dynamic-slice_bitcast_fusion.4
  79.6 2.0 %gather_fusion = f32[32,128,128]{2,1,0:T(8,128)} fusion(f32[8,128,128]{2,1,0:T(8,128)S(1)} %dynamic-slice_bitcast_fusion.4, s32[1024]{0:T(1024)S(1)} %get-tuple-element.158), kind=kCustom, calls=%fused_computation.1.clone.1 | custom fusion | bytes 4194432 | tf_op jit(solution)/shard_map/while/body/eval_jaxpr/jit(_take)/gather | solution.py:11
  81.6 2.0 %gather_fusion.1 = f32[32,128,128]{2,1,0:T(8,128)} fusion(f32[4,128,128]{2,1,0:T(8,128)S(1)} %dynamic-slice_bitcast_fusion.5, s32[1024]{0:T(1024)S(1)} %get-tuple-element.159), kind=kCustom, calls=%fused_computation.clone.1 | custom fusion | bytes 4194432 | tf_op jit(solution)/shard_map/while/body/eval_jaxpr/jit(_take)/gather | solution.py:10
  83.6 4.6 %fusion.17 = f32[32,128,128]{2,1,0:T(8,128)S(1)} fusion(f32[32,128,128]{2,1,0:T(8,128)} %gather_fusion, f32[32,128,128]{2,1,0:T(8,128)} %gather_fusion.1, pred[32]{0:T(512)(128)(4,1)S(1)} %get-tuple-element.160, pred[32]{0:T(512)(128)(4,1)S(1)} %get-tuple-element.161), kind=kOutput, calls=%fused_computation.3.clone.1 | convolution fusion | flops 806354944 | bytes 6291520 | tf_op jit(solution)/shard_map/while/body/eval_jaxpr/qxy,qyz->qxz/dot_general | solution.py:12
  88.2 5.9 %scatter_fusion = f32[32,128,128]{2,1,0:T(8,128)} fusion(f32[32,128,128]{2,1,0:T(8,128)} %get-tuple-element.169, s32[32]{0:T(128)S(1)} %get-tuple-element.155, f32[32,128,128]{2,1,0:T(8,128)S(1)} %fusion.17), kind=kCustom, calls=%fused_computation.2.clone.1 | custom fusion | flops 524288 | bytes 6291584 | tf_op jit(solution)/shard_map/while/body/eval_jaxpr/scatter-add | solution.py:19
  94.2 1.0 dynamic-slice_bitcast_fusion.5
  95.2 1.1 dynamic-slice_bitcast_fusion.4
  96.3 2.0 %gather_fusion = f32[32,128,128]{2,1,0:T(8,128)} fusion(f32[8,128,128]{2,1,0:T(8,128)S(1)} %dynamic-slice_bitcast_fusion.4, s32[1024]{0:T(1024)S(1)} %get-tuple-element.158), kind=kCustom, calls=%fused_computation.1.clone.1 | custom fusion | bytes 4194432 | tf_op jit(solution)/shard_map/while/body/eval_jaxpr/jit(_take)/gather | solution.py:11
  98.3 2.0 %gather_fusion.1 = f32[32,128,128]{2,1,0:T(8,128)} fusion(f32[4,128,128]{2,1,0:T(8,128)S(1)} %dynamic-slice_bitcast_fusion.5, s32[1024]{0:T(1024)S(1)} %get-tuple-element.159), kind=kCustom, calls=%fused_computation.clone.1 | custom fusion | bytes 4194432 | tf_op jit(solution)/shard_map/while/body/eval_jaxpr/jit(_take)/gather | solution.py:10
  100.3 4.6 %fusion.17 = f32[32,128,128]{2,1,0:T(8,128)S(1)} fusion(f32[32,128,128]{2,1,0:T(8,128)} %gather_fusion, f32[32,128,128]{2,1,0:T(8,128)} %gather_fusion.1, pred[32]{0:T(512)(128)(4,1)S(1)} %get-tuple-element.160, pred[32]{0:T(512)(128)(4,1)S(1)} %get-tuple-element.161), kind=kOutput, calls=%fused_computation.3.clone.1 | convolution fusion | flops 806354944 | bytes 6291520 | tf_op jit(solution)/shard_map/while/body/eval_jaxpr/qxy,qyz->qxz/dot_general | solution.py:12
  104.8 5.9 %scatter_fusion = f32[32,128,128]{2,1,0:T(8,128)} fusion(f32[32,128,128]{2,1,0:T(8,128)} %get-tuple-element.169, s32[32]{0:T(128)S(1)} %get-tuple-element.155, f32[32,128,128]{2,1,0:T(8,128)S(1)} %fusion.17), kind=kCustom, calls=%fused_computation.2.clone.1 | custom fusion | flops 524288 | bytes 6291584 | tf_op jit(solution)/shard_map/while/body/eval_jaxpr/scatter-add | solution.py:19
  110.8 1.0 dynamic-slice_bitcast_fusion.5
  111.8 1.1 dynamic-slice_bitcast_fusion.4
  112.9 2.0 %gather_fusion = f32[32,128,128]{2,1,0:T(8,128)} fusion(f32[8,128,128]{2,1,0:T(8,128)S(1)} %dynamic-slice_bitcast_fusion.4, s32[1024]{0:T(1024)S(1)} %get-tuple-element.158), kind=kCustom, calls=%fused_computation.1.clone.1 | custom fusion | bytes 4194432 | tf_op jit(solution)/shard_map/while/body/eval_jaxpr/jit(_take)/gather | solution.py:11
  114.9 2.0 %gather_fusion.1 = f32[32,128,128]{2,1,0:T(8,128)} fusion(f32[4,128,128]{2,1,0:T(8,128)S(1)} %dynamic-slice_bitcast_fusion.5, s32[1024]{0:T(1024)S(1)} %get-tuple-element.159), kind=kCustom, calls=%fused_computation.clone.1 | custom fusion | bytes 4194432 | tf_op jit(solution)/shard_map/while/body/eval_jaxpr/jit(_take)/gather | solution.py:10
  116.9 4.6 %fusion.17 = f32[32,128,128]{2,1,0:T(8,128)S(1)} fusion(f32[32,128,128]{2,1,0:T(8,128)} %gather_fusion, f32[32,128,128]{2,1,0:T(8,128)} %gather_fusion.1, pred[32]{0:T(512)(128)(4,1)S(1)} %get-tuple-element.160, pred[32]{0:T(512)(128)(4,1)S(1)} %get-tuple-element.161), kind=kOutput, calls=%fused_computation.3.clone.1 | convolution fusion | flops 806354944 | bytes 6291520 | tf_op jit(solution)/shard_map/while/body/eval_jaxpr/qxy,qyz->qxz/dot_general | solution.py:12
  121.4 5.9 %scatter_fusion = f32[32,128,128]{2,1,0:T(8,128)} fusion(f32[32,128,128]{2,1,0:T(8,128)} %get-tuple-element.169, s32[32]{0:T(128)S(1)} %get-tuple-element.155, f32[32,128,128]{2,1,0:T(8,128)S(1)} %fusion.17), kind=kCustom, calls=%fused_computation.2.clone.1 | custom fusion | flops 524288 | bytes 6291584 | tf_op jit(solution)/shard_map/while/body/eval_jaxpr/scatter-add | solution.py:19
  127.4 1.0 dynamic-slice_bitcast_fusion.5
  128.4 1.1 dynamic-slice_bitcast_fusion.4
  129.5 2.0 %gather_fusion = f32[32,128,128]{2,1,0:T(8,128)} fusion(f32[8,128,128]{2,1,0:T(8,128)S(1)} %dynamic-slice_bitcast_fusion.4, s32[1024]{0:T(1024)S(1)} %get-tuple-element.158), kind=kCustom, calls=%fused_computation.1.clone.1 | custom fusion | bytes 4194432 | tf_op jit(solution)/shard_map/while/body/eval_jaxpr/jit(_take)/gather | solution.py:11
  131.5 2.0 %gather_fusion.1 = f32[32,128,128]{2,1,0:T(8,128)} fusion(f32[4,128,128]{2,1,0:T(8,128)S(1)} %dynamic-slice_bitcast_fusion.5, s32[1024]{0:T(1024)S(1)} %get-tuple-element.159), kind=kCustom, calls=%fused_computation.clone.1 | custom fusion | bytes 4194432 | tf_op jit(solution)/shard_map/while/body/eval_jaxpr/jit(_take)/gather | solution.py:10
  133.5 4.6 %fusion.17 = f32[32,128,128]{2,1,0:T(8,128)S(1)} fusion(f32[32,128,128]{2,1,0:T(8,128)} %gather_fusion, f32[32,128,128]{2,1,0:T(8,128)} %gather_fusion.1, pred[32]{0:T(512)(128)(4,1)S(1)} %get-tuple-element.160, pred[32]{0:T(512)(128)(4,1)S(1)} %get-tuple-element.161), kind=kOutput, calls=%fused_computation.3.clone.1 | convolution fusion | flops 806354944 | bytes 6291520 | tf_op jit(solution)/shard_map/while/body/eval_jaxpr/qxy,qyz->qxz/dot_general | solution.py:12
  138.1 5.9 %scatter_fusion = f32[32,128,128]{2,1,0:T(8,128)} fusion(f32[32,128,128]{2,1,0:T(8,128)} %get-tuple-element.169, s32[32]{0:T(128)S(1)} %get-tuple-element.155, f32[32,128,128]{2,1,0:T(8,128)S(1)} %fusion.17), kind=kCustom, calls=%fused_computation.2.clone.1 | custom fusion | flops 524288 | bytes 6291584 | tf_op jit(solution)/shard_map/while/body/eval_jaxpr/scatter-add | solution.py:19
  144.0 0.0 reduce-scatter.2.cloned.1.call-update
  144.0 31.5 %reduce-scatter.2.cloned.1.call-done = f32[16,128,128]{2,1,0:T(8,128)} async-done(((f32[32,128,128]{2,1,0:T(8,128)}), f32[16,128,128]{2,1,0:T(8,128)}) %reduce-scatter.2.cloned.1.call-update) | async-done | bytes 1048592 | tf_op jit(solution)/shard_map/reduce_scatter | solution.py:45
  (16 shorter events, 0.1 us)
Async XLA Ops:
  6.5 21.8 %all-gather.5.cloned.1.call-start = ((), (), s32[]{:S(2)}) async-start(), calls=%async_computation.2 | async-start | bytes 1310720 | tf_op jit(solution)/shard_map/all_gather | solution.py:36
  7.3 68.7 %all-gather.7.cloned.1.call-start = ((), (), s32[]{:S(2)}) async-start(), calls=%async_computation.3 | async-start | bytes 2621440 | tf_op jit(solution)/shard_map/all_gather | solution.py:35
  8.0 167.5 %reduce-scatter.2.cloned.1.call-start = ((), (), s32[]{:S(2)}) async-start(), calls=%async_computation.1 | async-start | bytes 3145728 | tf_op jit(solution)/shard_map/reduce_scatter | solution.py:45
Sparse Core Ops, SparseCore 0:
  8.9 19.4 all-gather.4
  29.9 45.9 all-gather.6
  144.1 31.3 reduce-scatter.1
where the time goes:
time: 183 us; the launch traced here: 182 us
  waiting for transfers between devices  100 us (55%)
  local copies, waits for them, and re-layouts  26.5 us (14%)
  other arithmetic  23.7 us (13%)
  matrix products  18.2 us (10%)
  between operations  13.1 us (7%)
    all_gather x1, waiting for transfers between devices, body(): right_whole = lax.all_gather(right_local, 'row', axis=0, tiled=True)  47.5 us
    reduce_scatter x1, waiting for transfers between devices, body(): lax.psum_scatter(accumulated, 'layer', scatter_dimension=0, tiled=True)  31.5 us
    scatter-add x4, other arithmetic, multiply(): return running.at[out_slot].add(products, mode='drop')  23.7 us
    all_gather x1, waiting for transfers between devices, body(): pieces = lax.all_gather(left_local, 'col', axis=0, tiled=True)  19.6 us
    dot_general x4, matrix products, multiply(): jnp.einsum('qxy,qyz->qxz', first_blocks, second_blocks, precision=lax.Pre...  18.2 us
    gather x4, local copies, waits for them, and re-layouts, multiply(): first_blocks = jnp.take(left_piece, left_slot, axis=0)  8.03 us
    gather x4, local copies, waits for them, and re-layouts, multiply(): second_blocks = jnp.take(right_piece, right_slot, axis=0)  7.96 us
    squeeze x4, local copies, waits for them, and re-layouts, visit(): lax.dynamic_index_in_dim(right_whole, position, 0, keepdims=False)  4.33 us
  transfers between devices with their start and end apart: 3, of which 3 were waited for; matrix products, arithmetic and copies ran while one was open for 0% of the time, Pallas kernels for 0%

commit v1 on v0

--- a/solution.py
+++ b/solution.py
@@ -32,7 +32,12 @@
     stacks = pair_stacks[0, 0, 0]
     block_width = left_local.shape[-1]
     initial = jnp.zeros((OUT_TILE, block_width, block_width), jnp.float32)
-    right_whole = lax.all_gather(right_local, "row", axis=0, tiled=True)
+    ring = [right_local]
+    for hop in range(3):
+        ring.append(lax.ppermute(ring[-1], "row", [(dev, (dev + 1) % 4) for dev in range(4)]))
+    right_whole = jnp.roll(
+        jnp.concatenate(ring[::-1], axis=0), (lax.axis_index("row") + 1) * ring[0].shape[0], axis=0
+    )
     pieces = lax.all_gather(left_local, "col", axis=0, tiled=True)
 
     def visit(position, running):

time: 183 us -> 166 us (0.907)
  waiting for transfers between devices: 100 us -> 77.4 us
  starting transfers between devices: 0.08 us -> 3.07 us
    all_gather x1 -> x0, waiting for transfers between devices: 47.5 us -> none  [body(): right_whole = lax.all_gather(right_local, 'row', axis=0, tiled=True)]
    ppermute x0 -> x3, waiting for transfers between devices: none -> 42.3 us  [body(): lax.ppermute(ring[-1], 'row', [(dev, (dev + 1) % 4) for dev in range(4)])]
    all_gather x1, waiting for transfers between devices: 19.6 us -> 2.36 us  [body(): pieces = lax.all_gather(left_local, 'col', axis=0, tiled=True)]
    ppermute x0 -> x3, starting transfers between devices: none -> 3.03 us  [body(): lax.ppermute(ring[-1], 'row', [(dev, (dev + 1) % 4) for dev in range(4)])]
  transfers between devices with their start and end apart: 3 -> 5, of which waited for: 3 -> 5; matrix products, arithmetic and copies ran while one was open for 0% -> 2% of each run, Pallas kernels for 0% -> 0%
where the time goes in v1:
time: 166 us; the launch traced here: 165 us
  waiting for transfers between devices  77.4 us (47%)
  local copies, waits for them, and re-layouts  28.3 us (17%)
  other arithmetic  23.8 us (14%)
  matrix products  18.2 us (11%)
  between operations  13.5 us (8%)
  starting transfers between devices  3.07 us (2%)
    ppermute x3, waiting for transfers between devices, body(): lax.ppermute(ring[-1], 'row', [(dev, (dev + 1) % 4) for dev in range(4)])  42.3 us
    reduce_scatter x1, waiting for transfers between devices, body(): lax.psum_scatter(accumulated, 'layer', scatter_dimension=0, tiled=True)  32.7 us
    scatter-add x4, other arithmetic, multiply(): return running.at[out_slot].add(products, mode='drop')  23.8 us
    dot_general x4, matrix products, multiply(): jnp.einsum('qxy,qyz->qxz', first_blocks, second_blocks, precision=lax.Pre...  18.2 us
    gather x4, local copies, waits for them, and re-layouts, multiply(): first_blocks = jnp.take(left_piece, left_slot, axis=0)  8.02 us
    gather x4, local copies, waits for them, and re-layouts, multiply(): second_blocks = jnp.take(right_piece, right_slot, axis=0)  7.94 us
    squeeze x4, local copies, waits for them, and re-layouts, visit(): lax.dynamic_index_in_dim(right_whole, position, 0, keepdims=False)  4.33 us
    squeeze x4, local copies, waits for them, and re-layouts, visit(): left_piece = lax.dynamic_index_in_dim(pieces, position, 0, keepdims=False)  3.87 us
  transfers between devices with their start and end apart: 5, of which 5 were waited for; matrix products, arithmetic and copies ran while one was open for 2% of the time, Pallas kernels for 0%

profile of v1, /device:TPU:0, one launch (start us, length us, event | category | flops | bytes accessed | tf_op | source)
XLA Modules:
  0.0 164.5 jit_solution(3467298692775811031)
XLA Ops:
  6.5 0.0 copy-start
  6.5 0.0 all-gather.3.cloned.1.call-start
  6.5 3.0 %collective-permute-start = (f32[1,8,128,128]{3,2,1,0:T(8,128)}, f32[1,8,128,128]{3,2,1,0:T(8,128)S(1)}, u32[]{:S(2)}, u32[]{:S(2)}) collective-permute-start(f32[1,8,128,128]{3,2,1,0:T(8,128)} %bitcast.38), channel_id=1, source_target_pairs={{0,8},{8,16},{16,24},{24,0},{1,9},{9,17},{17,25},{25,1},{2,10},{10... | collective-permute-start | bytes 1572872 | tf_op jit(solution)/shard_map/ppermute | solution.py:37
  9.6 14.2 %collective-permute-done = f32[1,8,128,128]{3,2,1,0:T(8,128)S(1)} collective-permute-done((f32[1,8,128,128]{3,2,1,0:T(8,128)}, f32[1,8,128,128]{3,2,1,0:T(8,128)S(1)}, u32[]{:S(2)}, u32[]{:S(2)}) %collective-permute-start) | collective-permute-done | bytes 524320 | tf_op jit(solution)/shard_map/ppermute | solution.py:37
  23.8 0.0 collective-permute-start.1
  23.8 14.9 %collective-permute-done.1 = f32[1,8,128,128]{3,2,1,0:T(8,128)S(1)} collective-permute-done((f32[1,8,128,128]{3,2,1,0:T(8,128)S(1)}, f32[1,8,128,128]{3,2,1,0:T(8,128)S(1)}, u32[]{:S(2)}, u32[]{:S(2)}) %collective-permute-start.1) | collective-permute-done | bytes 524320 | tf_op jit(solution)/shard_map/ppermute | solution.py:37
  38.7 0.0 collective-permute-start.2
  38.7 0.0 all-gather.3.cloned.1.call-update
  38.7 0.0 reduce-scatter.2.cloned.1.call-start
  38.8 0.7 copy.8
  39.5 13.2 %collective-permute-done.2 = f32[1,8,128,128]{3,2,1,0:T(8,128)S(1)} collective-permute-done((f32[1,8,128,128]{3,2,1,0:T(8,128)S(1)}, f32[1,8,128,128]{3,2,1,0:T(8,128)S(1)}, u32[]{:S(2)}, u32[]{:S(2)}) %collective-permute-start.2) | collective-permute-done | bytes 524320 | tf_op jit(solution)/shard_map/ppermute | solution.py:37
  52.8 0.0 copy-done
  53.0 1.5 constant_dynamic-slice_fusion.1
  54.5 2.4 %all-gather.3.cloned.1.call-done = f32[4,1,1,4,128,128]{5,4,3,2,1,0:T(8,128)} async-done(((f32[1,1,1,4,128,128]{5,4,3,2,1,0:T(8,128)}), f32[4,1,1,4,128,128]{5,4,3,2,1,0:T(8,128)}) %all-gather.3.cloned.1.call-update) | async-done | bytes 1048592 | tf_op jit(solution)/shard_map/all_gather | solution.py:41
  56.9 1.6 broadcast_in_dim.43
  58.5 66.5 %while.13 = (s32[]{:T(128)}, f32[32,128,128]{2,1,0:T(8,128)}, s32[4,3,32]{2,1,0:T(4,128)S(1)}, f32[4,4,128,128]{3,2,1,0:T(8,128)}, f32[4,8,128,128]{3,2,1,0:T(8,128)}, /*index=5*/s32[]{:T(128)}) while((s32[]{:T(128)}, f32[32,128,128]{2,1,0:T(8,128)}, s32[4,3,32]{2,1,0:T(4,128)S(1)}, f32[4,4,128,128]{3,2,1,0:T(8,128)}, ...), condition=%wide.region_2.3_spmd, body=%wide.region_0.2_spmd.sunk | while | flops 806881984 | bytes 22555216 | solution.py:49
  58.5 1.1 dynamic-slice_bitcast_fusion.4
  59.6 2.0 %gather_fusion = f32[32,128,128]{2,1,0:T(8,128)} fusion(f32[8,128,128]{2,1,0:T(8,128)S(1)} %dynamic-slice_bitcast_fusion.4, s32[1024]{0:T(1024)S(1)} %get-tuple-element.158), kind=kCustom, calls=%fused_computation.1.clone.1 | custom fusion | bytes 4194432 | tf_op jit(solution)/shard_map/while/body/eval_jaxpr/jit(_take)/gather | solution.py:11
  61.6 1.0 dynamic-slice_bitcast_fusion.5
  62.6 2.0 %gather_fusion.1 = f32[32,128,128]{2,1,0:T(8,128)} fusion(f32[4,128,128]{2,1,0:T(8,128)S(1)} %dynamic-slice_bitcast_fusion.5, s32[1024]{0:T(1024)S(1)} %get-tuple-element.159), kind=kCustom, calls=%fused_computation.clone.1 | custom fusion | bytes 4194432 | tf_op jit(solution)/shard_map/while/body/eval_jaxpr/jit(_take)/gather | solution.py:10
  64.6 4.6 %fusion.17 = f32[32,128,128]{2,1,0:T(8,128)S(1)} fusion(f32[32,128,128]{2,1,0:T(8,128)} %gather_fusion, f32[32,128,128]{2,1,0:T(8,128)} %gather_fusion.1, pred[32]{0:T(512)(128)(4,1)S(1)} %get-tuple-element.160, pred[32]{0:T(512)(128)(4,1)S(1)} %get-tuple-element.161), kind=kOutput, calls=%fused_computation.3.clone.1 | convolution fusion | flops 806354944 | bytes 6291520 | tf_op jit(solution)/shard_map/while/body/eval_jaxpr/qxy,qyz->qxz/dot_general | solution.py:12
  69.1 6.0 %scatter_fusion = f32[32,128,128]{2,1,0:T(8,128)} fusion(f32[32,128,128]{2,1,0:T(8,128)} %get-tuple-element.169, s32[32]{0:T(128)S(1)} %get-tuple-element.155, f32[32,128,128]{2,1,0:T(8,128)S(1)} %fusion.17), kind=kCustom, calls=%fused_computation.2.clone.1 | custom fusion | flops 524288 | bytes 6291584 | tf_op jit(solution)/shard_map/while/body/eval_jaxpr/scatter-add | solution.py:19
  75.2 1.1 dynamic-slice_bitcast_fusion.4
  76.2 2.0 %gather_fusion = f32[32,128,128]{2,1,0:T(8,128)} fusion(f32[8,128,128]{2,1,0:T(8,128)S(1)} %dynamic-slice_bitcast_fusion.4, s32[1024]{0:T(1024)S(1)} %get-tuple-element.158), kind=kCustom, calls=%fused_computation.1.clone.1 | custom fusion | bytes 4194432 | tf_op jit(solution)/shard_map/while/body/eval_jaxpr/jit(_take)/gather | solution.py:11
  78.2 1.0 dynamic-slice_bitcast_fusion.5
  79.2 2.0 %gather_fusion.1 = f32[32,128,128]{2,1,0:T(8,128)} fusion(f32[4,128,128]{2,1,0:T(8,128)S(1)} %dynamic-slice_bitcast_fusion.5, s32[1024]{0:T(1024)S(1)} %get-tuple-element.159), kind=kCustom, calls=%fused_computation.clone.1 | custom fusion | bytes 4194432 | tf_op jit(solution)/shard_map/while/body/eval_jaxpr/jit(_take)/gather | solution.py:10
  81.2 4.6 %fusion.17 = f32[32,128,128]{2,1,0:T(8,128)S(1)} fusion(f32[32,128,128]{2,1,0:T(8,128)} %gather_fusion, f32[32,128,128]{2,1,0:T(8,128)} %gather_fusion.1, pred[32]{0:T(512)(128)(4,1)S(1)} %get-tuple-element.160, pred[32]{0:T(512)(128)(4,1)S(1)} %get-tuple-element.161), kind=kOutput, calls=%fused_computation.3.clone.1 | convolution fusion | flops 806354944 | bytes 6291520 | tf_op jit(solution)/shard_map/while/body/eval_jaxpr/qxy,qyz->qxz/dot_general | solution.py:12
  85.8 5.9 %scatter_fusion = f32[32,128,128]{2,1,0:T(8,128)} fusion(f32[32,128,128]{2,1,0:T(8,128)} %get-tuple-element.169, s32[32]{0:T(128)S(1)} %get-tuple-element.155, f32[32,128,128]{2,1,0:T(8,128)S(1)} %fusion.17), kind=kCustom, calls=%fused_computation.2.clone.1 | custom fusion | flops 524288 | bytes 6291584 | tf_op jit(solution)/shard_map/while/body/eval_jaxpr/scatter-add | solution.py:19
  91.8 1.1 dynamic-slice_bitcast_fusion.4
  92.9 2.0 %gather_fusion = f32[32,128,128]{2,1,0:T(8,128)} fusion(f32[8,128,128]{2,1,0:T(8,128)S(1)} %dynamic-slice_bitcast_fusion.4, s32[1024]{0:T(1024)S(1)} %get-tuple-element.158), kind=kCustom, calls=%fused_computation.1.clone.1 | custom fusion | bytes 4194432 | tf_op jit(solution)/shard_map/while/body/eval_jaxpr/jit(_take)/gather | solution.py:11
  94.8 1.0 dynamic-slice_bitcast_fusion.5
  95.8 2.0 %gather_fusion.1 = f32[32,128,128]{2,1,0:T(8,128)} fusion(f32[4,128,128]{2,1,0:T(8,128)S(1)} %dynamic-slice_bitcast_fusion.5, s32[1024]{0:T(1024)S(1)} %get-tuple-element.159), kind=kCustom, calls=%fused_computation.clone.1 | custom fusion | bytes 4194432 | tf_op jit(solution)/shard_map/while/body/eval_jaxpr/jit(_take)/gather | solution.py:10
  97.8 4.6 %fusion.17 = f32[32,128,128]{2,1,0:T(8,128)S(1)} fusion(f32[32,128,128]{2,1,0:T(8,128)} %gather_fusion, f32[32,128,128]{2,1,0:T(8,128)} %gather_fusion.1, pred[32]{0:T(512)(128)(4,1)S(1)} %get-tuple-element.160, pred[32]{0:T(512)(128)(4,1)S(1)} %get-tuple-element.161), kind=kOutput, calls=%fused_computation.3.clone.1 | convolution fusion | flops 806354944 | bytes 6291520 | tf_op jit(solution)/shard_map/while/body/eval_jaxpr/qxy,qyz->qxz/dot_general | solution.py:12
  102.4 5.9 %scatter_fusion = f32[32,128,128]{2,1,0:T(8,128)} fusion(f32[32,128,128]{2,1,0:T(8,128)} %get-tuple-element.169, s32[32]{0:T(128)S(1)} %get-tuple-element.155, f32[32,128,128]{2,1,0:T(8,128)S(1)} %fusion.17), kind=kCustom, calls=%fused_computation.2.clone.1 | custom fusion | flops 524288 | bytes 6291584 | tf_op jit(solution)/shard_map/while/body/eval_jaxpr/scatter-add | solution.py:19
  108.4 1.1 dynamic-slice_bitcast_fusion.4
  109.5 2.0 %gather_fusion = f32[32,128,128]{2,1,0:T(8,128)} fusion(f32[8,128,128]{2,1,0:T(8,128)S(1)} %dynamic-slice_bitcast_fusion.4, s32[1024]{0:T(1024)S(1)} %get-tuple-element.158), kind=kCustom, calls=%fused_computation.1.clone.1 | custom fusion | bytes 4194432 | tf_op jit(solution)/shard_map/while/body/eval_jaxpr/jit(_take)/gather | solution.py:11
  111.5 1.0 dynamic-slice_bitcast_fusion.5
  112.4 2.0 %gather_fusion.1 = f32[32,128,128]{2,1,0:T(8,128)} fusion(f32[4,128,128]{2,1,0:T(8,128)S(1)} %dynamic-slice_bitcast_fusion.5, s32[1024]{0:T(1024)S(1)} %get-tuple-element.159), kind=kCustom, calls=%fused_computation.clone.1 | custom fusion | bytes 4194432 | tf_op jit(solution)/shard_map/while/body/eval_jaxpr/jit(_take)/gather | solution.py:10
  114.5 4.6 %fusion.17 = f32[32,128,128]{2,1,0:T(8,128)S(1)} fusion(f32[32,128,128]{2,1,0:T(8,128)} %gather_fusion, f32[32,128,128]{2,1,0:T(8,128)} %gather_fusion.1, pred[32]{0:T(512)(128)(4,1)S(1)} %get-tuple-element.160, pred[32]{0:T(512)(128)(4,1)S(1)} %get-tuple-element.161), kind=kOutput, calls=%fused_computation.3.clone.1 | convolution fusion | flops 806354944 | bytes 6291520 | tf_op jit(solution)/shard_map/while/body/eval_jaxpr/qxy,qyz->qxz/dot_general | solution.py:12
  119.0 5.9 %scatter_fusion = f32[32,128,128]{2,1,0:T(8,128)} fusion(f32[32,128,128]{2,1,0:T(8,128)} %get-tuple-element.169, s32[32]{0:T(128)S(1)} %get-tuple-element.155, f32[32,128,128]{2,1,0:T(8,128)S(1)} %fusion.17), kind=kCustom, calls=%fused_computation.2.clone.1 | custom fusion | flops 524288 | bytes 6291584 | tf_op jit(solution)/shard_map/while/body/eval_jaxpr/scatter-add | solution.py:19
  125.0 0.0 reduce-scatter.2.cloned.1.call-update
  125.0 32.7 %reduce-scatter.2.cloned.1.call-done = f32[16,128,128]{2,1,0:T(8,128)} async-done(((f32[32,128,128]{2,1,0:T(8,128)}), f32[16,128,128]{2,1,0:T(8,128)}) %reduce-scatter.2.cloned.1.call-update) | async-done | bytes 1048592 | tf_op jit(solution)/shard_map/reduce_scatter | solution.py:50
  (24 shorter events, 0.4 us)
Async XLA Ops:
  6.5 46.3 %copy-start = (f32[1,1,1,8,128,128]{5,4,3,2,1,0:T(8,128)S(1)}, f32[1,1,1,8,128,128]{5,4,3,2,1,0:T(8,128)}, u32[]{:S(2)}) copy-start(f32[1,1,1,8,128,128]{5,4,3,2,1,0:T(8,128)} %param.6) | copy-start | bytes 1572868
  6.5 50.4 %all-gather.3.cloned.1.call-start = ((), (), s32[]{:S(2)}) async-start(), calls=%async_computation.2 | async-start | bytes 1310720 | tf_op jit(solution)/shard_map/all_gather | solution.py:41
  6.5 17.2 %collective-permute-start = (f32[1,8,128,128]{3,2,1,0:T(8,128)}, f32[1,8,128,128]{3,2,1,0:T(8,128)S(1)}, u32[]{:S(2)}, u32[]{:S(2)}) collective-permute-start(f32[1,8,128,128]{3,2,1,0:T(8,128)} %bitcast.38), channel_id=1, source_target_pairs={{0,8},{8,16},{16,24},{24,0},{1,9},{9,17},{17,25},{25,1},{2,10},{10... | collective-permute-start | bytes 1572872 | tf_op jit(solution)/shard_map/ppermute | solution.py:37
  23.8 14.9 %collective-permute-start.1 = (f32[1,8,128,128]{3,2,1,0:T(8,128)S(1)}, f32[1,8,128,128]{3,2,1,0:T(8,128)S(1)}, u32[]{:S(2)}, u32[]{:S(2)}) collective-permute-start(f32[1,8,128,128]{3,2,1,0:T(8,128)S(1)} %collective-permute-done), channel_id=1, source_target_pairs={{0,8},{8,16},{16,24},{24,0},{1,9},{9,17},{17,25},{25,1},{2,10},{10... | collective-permute-start | bytes 1572872 | tf_op jit(solution)/shard_map/ppermute | solution.py:37
  38.7 14.0 %collective-permute-start.2 = (f32[1,8,128,128]{3,2,1,0:T(8,128)S(1)}, f32[1,8,128,128]{3,2,1,0:T(8,128)S(1)}, u32[]{:S(2)}, u32[]{:S(2)}) collective-permute-start(f32[1,8,128,128]{3,2,1,0:T(8,128)S(1)} %collective-permute-done.1), channel_id=1, source_target_pairs={{0,8},{8,16},{16,24},{24,0},{1,9},{9,17},{17,25},{25,1},{2,10},{10... | collective-permute-start | bytes 1572872 | tf_op jit(solution)/shard_map/ppermute | solution.py:37
  38.7 119.0 %reduce-scatter.2.cloned.1.call-start = ((), (), s32[]{:S(2)}) async-start(), calls=%async_computation.1 | async-start | bytes 3145728 | tf_op jit(solution)/shard_map/reduce_scatter | solution.py:50
Sparse Core Ops, SparseCore 0:
  38.8 18.0 all-gather.2
  125.1 32.5 reduce-scatter.1
